TPU v7x, 256 devices: a whole 4x4x8 slice. The times are simulated.
256 devices in a mesh: src: 16 (over x, y), tgt: 16 (over z, core).
Axes of the slice: x: 4, y: 4, z: 8, core: 2. Of those that a mesh axis runs over, the one named last changes fastest.
Arguments:
- src_codes: bfloat16 [1024, 24576], P('tgt', 'src'), may hold values from -1 to 1
- src_scale: float32 [24576], P('src'), may hold values from 0.8 to 1.25
- tgt_codes: bfloat16 [1024, 16384], P('src', 'tgt'), may hold values from -1 to 1
- tgt_scale: float32 [16384], P('tgt'), may hold values from 0.8 to 1.25
Outputs:
- forward_best: float32 [4, 24576], P(None, 'src')
- backward_best: float32 [4, 16384], P(None, 'tgt')
All inputs are finite; a program needn't handle non-finite values.
Results may differ from a plain program's by a relative error of at most 0.0003.
Values may be sent and summed in bfloat16 or wider, within the bound.
A program may use at most 64 MiB of HBM per device.

v0:
```python
import jax
import jax.numpy as jnp
from jax import lax
from jax.sharding import PartitionSpec as P

KNN = 4
KEEP = 4


def combined_all(part, axis, combine):
    gathered = jax.tree.map(lambda a: lax.all_gather(a, axis), part)

    def take(source):
        return jax.tree.map(lambda a: lax.dynamic_index_in_dim(a, source, 0, False), gathered)

    return lax.fori_loop(
        1, lax.axis_size(axis), lambda source, state: combine(state, take(source)), take(0)
    )


def tile_scores(block, block_scale, targets, target_scale):
    dots = lax.dot_general(
        block, targets, (((0,), (0,)), ((), ())), preferred_element_type=jnp.float32
    )
    return dots * block_scale[:, None] * target_scale[None, :]


def best_values(values, width, axis):
    places = lax.broadcasted_iota(jnp.int32, values.shape, axis)
    length = values.shape[axis]
    picked = []
    for _ in range(width):
        largest = jnp.max(values, axis=axis, keepdims=True)
        position = jnp.min(jnp.where(values == largest, places, length), axis=axis, keepdims=True)
        picked.append(jnp.squeeze(largest, axis))
        values = jnp.where(places == position, jnp.float32(-1e30), values)
    return jnp.stack(picked, axis=-1)


def merge_lists(first, second):
    return best_values(jnp.concatenate([first, second], axis=1), first.shape[1], 1)


def forward_lists(lists):
    return combined_all(lists, "tgt", merge_lists)


def backward_lists(lists):
    return combined_all(lists, "src", merge_lists)


def sweep(
    sources, source_scale, targets, target_scale, source_denom, target_denom, use_margin, width
):
    rows = sources.shape[1]
    step = 128
    count = rows // step
    items = (
        jnp.arange(count, dtype=jnp.int32),
        source_scale.reshape(count, step),
        source_denom.reshape(count, step),
    )

    def visit(carry, item):
        index, scale, denom = item
        block = lax.dynamic_slice_in_dim(sources, index * step, step, 1)
        sim = tile_scores(block, scale, targets, target_scale)
        if use_margin:
            sim = sim / (0.5 * (denom[:, None] + target_denom[None, :]))
        ahead = best_values(sim, width, 1)
        column = best_values(sim, width, 0)
        return (merge_lists(carry, column), ahead)

    start = jnp.full((targets.shape[1], width), -1e30, jnp.float32)
    behind, ahead = lax.scan(visit, start, items)
    return (ahead.reshape(rows, width), behind)


def body(src_codes, src_scale, tgt_codes, tgt_scale):
    sources = lax.all_gather(src_codes, "tgt", axis=0, tiled=True)
    targets = lax.all_gather(tgt_codes, "src", axis=0, tiled=True)
    dummy_src = jnp.ones_like(src_scale)
    dummy_tgt = jnp.ones_like(tgt_scale)
    ahead, behind = sweep(sources, src_scale, targets, tgt_scale, dummy_src, dummy_tgt, False, KNN)
    forward_knn = jnp.mean(forward_lists(ahead), axis=1)
    backward_knn = jnp.mean(backward_lists(behind), axis=1)
    best_ahead, best_behind = sweep(
        sources, src_scale, targets, tgt_scale, forward_knn, backward_knn, True, KEEP
    )
    final_ahead = forward_lists(best_ahead)
    final_behind = backward_lists(best_behind)
    return (final_ahead.T, final_behind.T)


def solution(mesh):
    placed = (P("tgt", "src"), P("src"), P("src", "tgt"), P("tgt"))
    return jax.shard_map(
        body,
        mesh=mesh,
        in_specs=placed,
        out_specs=(P(None, "src"), P(None, "tgt")),
        check_vma=False,
    )
```

profile of v0, /device:TPU:1, one launch (start us, length us, event | category | flops | bytes accessed | tf_op | source)
XLA Modules:
  0.0 374.5 jit_solution(13976334259187191952)
XLA Ops:
  8.6 54.7 %all-gather.7.cloned.1.call-done = bf16[1024,1024]{1,0:T(8,128)(2,1)} async-done(((bf16[64,1024]{1,0:T(8,128)(2,1)}), bf16[1024,1024]{1,0:T(8,128)(2,1)}) %all-gather.7.cloned.1.call-update) | async-done | bytes 2097168 | tf_op jit(solution)/shard_map/all_gather | solution.py:81
  63.4 43.5 %all-gather.5.cloned.1.call-done = bf16[1024,1536]{1,0:T(8,128)(2,1)} async-done(((bf16[64,1536]{1,0:T(8,128)(2,1)}), bf16[1024,1536]{1,0:T(8,128)(2,1)}) %all-gather.5.cloned.1.call-update) | async-done | bytes 3145744 | tf_op jit(solution)/shard_map/all_gather | solution.py:80
  106.9 77.0 %while.84 = (s32[]{:T(128)}, f32[1024,4]{0,1:T(4,128)S(1)}, f32[12,128,4]{1,2,0:T(4,128)S(1)}, s32[12]{0:T(128)S(1)}, bf16[1024,1536]{1,0:T(8,128)(2,1)}, /*inde...) while((s32[]{:T(128)}, f32[1024,4]{0,1:T(4,128)S(1)}, ...), condition=%wide.region_22.23_spmd, body=%wide.region_0.22_spmd.sunk | while | flops 277080704 | bytes 7613647 | solution.py:75
  108.8 2.1 fusion.82
  115.2 2.1 fusion.82
  121.6 2.1 fusion.82
  128.0 2.1 fusion.82
  134.4 2.1 fusion.82
  153.7 2.1 fusion.82
  160.1 2.1 fusion.82
  166.5 2.1 fusion.82
  183.9 18.5 %all-gather = f32[16384,4]{0,1:T(4,128)S(1)} all-gather(f32[1024,4]{0,1:T(4,128)S(1)} %get-tuple-element.452), channel_id=2, replica_groups=mesh['src'=16,'tgt'=16] {'src'}, dimensions={0}, use_global_device_ids=true | all-gather | bytes 278528 | tf_op jit(solution)/shard_map/all_gather | solution.py:11
  202.4 4.9 %while.86 = (s32[]{:T(128)}, f32[1024,4]{0,1:T(4,128)S(1)}, f32[16,1024,4]{1,2,0:T(4,128)S(1)}, s32[]{:T(128)}, s32[]{:T(128)}, /*index=5*/s32[]{:T(128)}, f32[]{:T(128)}) while((s32[]{:T(128)}, f32[1024,4]{0,1:T(4,128)S(1)}, f32[16,1024,4]{1,2,0:T(4,128)S(1)}, s32[]{:T(128)}, s32[]{:T(128)}, /*index=5*/s32[]{:T(128)}, f32[]{:T(128)}) %tuple.238), condition=%wide.region_43.44_spmd, body=%wide.region_34.43_spmd.sunk | while | flops 308229 | bytes 372855 | solution.py:16
  207.4 22.3 %all_gather.26 = f32[16,1536,4]{1,2,0:T(4,128)S(1)} all-gather(f32[1,1536,4]{1,2,0:T(4,128)S(1)} %bitcast.193), channel_id=1, replica_groups=mesh['src'=16,'tgt'=16] {'tgt'}, dimensions={0}, use_global_device_ids=true | all-gather | bytes 417792 | tf_op jit(solution)/shard_map/all_gather | solution.py:11
  229.7 6.9 %while.85 = (s32[]{:T(128)}, f32[1536,4]{0,1:T(4,128)S(1)}, f32[16,1536,4]{1,2,0:T(4,128)S(1)}, s32[]{:T(128)}, s32[]{:T(128)}, /*index=5*/s32[]{:T(128)}, f32[]{:T(128)}) while((s32[]{:T(128)}, f32[1536,4]{0,1:T(4,128)S(1)}, f32[16,1536,4]{1,2,0:T(4,128)S(1)}, s32[]{:T(128)}, s32[]{:T(128)}, /*index=5*/s32[]{:T(128)}, f32[]{:T(128)}) %tuple.217), condition=%wide.region_32.33_spmd, body=%wide.region_23.32_spmd.sunk | while | flops 462341 | bytes 608375 | solution.py:16
  236.7 80.1 %while.87 = (s32[]{:T(128)}, f32[1024,4]{0,1:T(4,128)S(1)}, f32[12,128,4]{1,2,0:T(4,128)S(1)}, s32[12]{0:T(128)S(1)}, bf16[1024,1536]{1,0:T(8,128)(2,1)}, /*inde...) while((s32[]{:T(128)}, f32[1024,4]{0,1:T(4,128)S(1)}, ...), condition=%wide.region_67.68_spmd, body=%wide.region_45.67_spmd.sunk | while | flops 277473920 | bytes 7619295 | solution.py:75
  238.8 2.3 fusion.94
  245.4 2.3 fusion.94
  252.1 2.3 fusion.94
  258.8 2.3 fusion.94
  265.5 2.3 fusion.94
  272.1 2.3 fusion.94
  278.8 2.3 fusion.94
  285.5 2.3 fusion.94
  292.1 2.3 fusion.94
  298.8 2.3 fusion.94
  305.5 2.3 fusion.94
  312.2 2.3 fusion.94
  316.8 17.9 %all-gather.1 = f32[16384,4]{0,1:T(4,128)S(1)} all-gather(f32[1024,4]{0,1:T(4,128)S(1)} %get-tuple-element.456), channel_id=3, replica_groups=mesh['src'=16,'tgt'=16] {'src'}, dimensions={0}, use_global_device_ids=true | all-gather | bytes 278528 | tf_op jit(solution)/shard_map/all_gather | solution.py:11
  334.7 4.9 %while.89 = (s32[]{:T(128)}, f32[1024,4]{0,1:T(4,128)S(1)}, f32[16,1024,4]{1,2,0:T(4,128)S(1)}, s32[]{:T(128)}, s32[]{:T(128)}, /*index=5*/s32[]{:T(128)}, f32[]{:T(128)}) while((s32[]{:T(128)}, f32[1024,4]{0,1:T(4,128)S(1)}, f32[16,1024,4]{1,2,0:T(4,128)S(1)}, s32[]{:T(128)}, s32[]{:T(128)}, /*index=5*/s32[]{:T(128)}, f32[]{:T(128)}) %tuple.239), condition=%wide.region_87.88_spmd, body=%wide.region_78.87_spmd.sunk | while | flops 308229 | bytes 372855 | solution.py:16
  339.6 20.5 %all_gather.29 = f32[16,1536,4]{1,2,0:T(4,128)S(1)} all-gather(f32[1,1536,4]{1,2,0:T(4,128)S(1)} %bitcast.192), channel_id=1, replica_groups=mesh['src'=16,'tgt'=16] {'tgt'}, dimensions={0}, use_global_device_ids=true | all-gather | bytes 417792 | tf_op jit(solution)/shard_map/all_gather | solution.py:11
  360.1 6.9 %while.88 = (s32[]{:T(128)}, f32[1536,4]{0,1:T(4,128)S(1)}, f32[16,1536,4]{1,2,0:T(4,128)S(1)}, s32[]{:T(128)}, s32[]{:T(128)}, /*index=5*/s32[]{:T(128)}, f32[]{:T(128)}) while((s32[]{:T(128)}, f32[1536,4]{0,1:T(4,128)S(1)}, f32[16,1536,4]{1,2,0:T(4,128)S(1)}, s32[]{:T(128)}, s32[]{:T(128)}, /*index=5*/s32[]{:T(128)}, f32[]{:T(128)}) %tuple.226), condition=%wide.region_77.78_spmd, body=%wide.region_68.77_spmd.sunk | while | flops 462341 | bytes 608375 | solution.py:16
  (1276 shorter events, 115.2 us)
Async XLA Ops:
  7.2 56.2 %all-gather.7.cloned.1.call-start = ((), (), s32[]{:S(2)}) async-start(), calls=%async_computation.1 | async-start | bytes 2228224 | tf_op jit(solution)/shard_map/all_gather | solution.py:81
  7.9 99.0 %all-gather.5.cloned.1.call-start = ((), (), s32[]{:S(2)}) async-start(), calls=%async_computation | async-start | bytes 3342336 | tf_op jit(solution)/shard_map/all_gather | solution.py:80
  207.3 29.4 %copy-start.2 = (f32[1024]{0:T(1024)S(1)}, f32[1024]{0:T(1024)}, u32[]{:S(2)}) copy-start(f32[1024]{0:T(1024)} %get-tuple-element.996) | copy-start | bytes 12292
  339.6 27.5 %copy-start.1 = (f32[1024,4]{0,1:T(4,128)}, f32[1024,4]{0,1:T(4,128)S(1)}, u32[]{:S(2)}) copy-start(f32[1024,4]{0,1:T(4,128)S(1)} %get-tuple-element.457) | copy-start | bytes 49156
  367.1 0.6 copy-start
Sparse Core Ops, SparseCore 0:
  10.4 52.8 all-gather.6
  65.2 41.6 all-gather.4
where the time goes:
time: 376 us; the launch traced here: 375 us
  waiting for transfers between devices  99.6 us (26%)
  blocking collectives  79.3 us (21%)
  other arithmetic  71.2 us (19%)
  matrix products  52.9 us (14%)
  local copies, waits for them, and re-layouts  34 us (9%)
  loops' own time  23.3 us (6%)
  between operations  14.2 us (4%)
    all_gather x4, blocking collectives, combined_all(): gathered = jax.tree.map(lambda a: lax.all_gather(a, axis), part)  79.3 us
    all_gather x1, waiting for transfers between devices, body(): targets = lax.all_gather(tgt_codes, 'src', axis=0, tiled=True)  54.7 us
    dot_general x24, matrix products, tile_scores(): lax.dot_general(block, targets, (((0,), (0,)), ((), ())), preferred_eleme...  52.9 us
    all_gather x1, waiting for transfers between devices, body(): sources = lax.all_gather(src_codes, 'tgt', axis=0, tiled=True)  43.5 us
    reduce_max x600, other arithmetic, best_values(): largest = jnp.max(values, axis=axis, keepdims=True)  35.5 us
    reduce_min x348, other arithmetic, best_values(): jnp.min(jnp.where(values == largest, places, length), axis=axis, keepdims...  33 us
    another operation x2, loops' own time, sweep(): behind, ahead = lax.scan(visit, start, items)  17.1 us
    mul x24, local copies, waits for them, and re-layouts, tile_scores(): return dots * block_scale[:, None] * target_scale[None, :]  16.8 us
  transfers between devices with their start and end apart: 2, of which 2 were waited for; matrix products, arithmetic and copies ran while one was open for 0% of the time, Pallas kernels for 0%

commit v1 on v0

v1 whole, which is shorter than its diff:
```python
import functools

import jax
import jax.numpy as jnp
from jax import lax
from jax.experimental import pallas as pl
from jax.experimental.pallas import tpu as pltpu
from jax.sharding import PartitionSpec as P

MESH = pl.DeviceIdType.MESH
F32 = jnp.float32
LOW = -1e30

NX, NY, NZ = 4, 4, 8
GROUP = 16
LANES = 128


def compare(a, b):
    return jnp.maximum(a, b), jnp.minimum(a, b)


def sort4(v):
    a, b = compare(v[0], v[1])
    c, d = compare(v[2], v[3])
    a, c = compare(a, c)
    b, d = compare(b, d)
    b, c = compare(b, c)
    return [a, b, c, d]


def merge4(p, q):
    a, b, c, d = [jnp.maximum(p[i], q[3 - i]) for i in range(4)]
    a, c = compare(a, c)
    b, d = compare(b, d)
    a, b = compare(a, b)
    c, d = compare(c, d)
    return [a, b, c, d]


def tree(lists):
    while len(lists) > 1:
        lists = [merge4(lists[i], lists[i + 1]) for i in range(0, len(lists), 2)]
    return lists[0]


def over_sublanes(best):
    for shift in (4, 2, 1):
        best = merge4(best, [pltpu.roll(v, shift, 0) for v in best])
    return best


def kernel(
    src_ref, src_scale, tgt_ref, tgt_scale, fwd_ref, bwd_ref,
    s_all, t_all, sim, side, lists, columns,
    row_out, row_in, row_mean, row_best,
    col_out, col_in, col_mean, col_best,
    own_sem, z_send, z_recv, d_send, d_recv, p_send, p_recv,
    g_send, g_recv, h_send, h_recv,
):
    src_me, tgt_me = lax.axis_index("src"), lax.axis_index("tgt")
    x, y = src_me // NY, lax.rem(src_me, NY)
    z, core = tgt_me // 2, lax.rem(tgt_me, 2)
    row_blocks, col_blocks = row_out.shape[0], col_out.shape[0]

    def around(v, step, n):
        return lax.rem(v + (step + n), n)

    def at_xy(dx, dy):
        return around(x, dx, NX) * NY + around(y, dy, NY)

    def at_z(dz):
        return around(z, dz, NZ) * 2 + core

    barrier = pltpu.get_barrier_semaphore()
    for r in range(1, GROUP):
        pl.semaphore_signal(
            barrier, inc=1, device_id=(src_me, around(tgt_me, r, GROUP)), device_id_type=MESH
        )
        pl.semaphore_signal(
            barrier, inc=1, device_id=(around(src_me, r, GROUP), tgt_me), device_id_type=MESH
        )

    own = []
    for h in range(2):
        part = pl.ds(h * 32, 32)
        own.append(pltpu.make_async_copy(src_ref.at[part], s_all.at[tgt_me, h], own_sem.at[0, h]))
        own.append(pltpu.make_async_copy(tgt_ref.at[part], t_all.at[src_me, h], own_sem.at[1, h]))
    for copy in own:
        copy.start()

    for b in range(row_blocks):
        line = src_scale[:, b * LANES:(b + 1) * LANES]
        side[b * LANES:(b + 1) * LANES, :] = jnp.broadcast_to(line, (LANES, LANES)).T
    columns[...] = jnp.full(columns.shape, LOW, F32)
    for copy in own:
        copy.wait()
    pl.semaphore_wait(barrier, 2 * (GROUP - 1))

    sent = []

    def z_copy(way, d, h):
        step = 1 if way == 0 else -1
        slot = s_all.at[at_z(-step * (d - 1)), h]
        return pltpu.make_async_remote_copy(
            src_ref=slot, dst_ref=slot,
            send_sem=z_send.at[way, d - 1, h], recv_sem=z_recv.at[way, d - 1, h],
            device_id=(src_me, at_z(step)), device_id_type=MESH,
        )

    def z_landed(way, d, h):
        step = 1 if way == 0 else -1
        slot = s_all.at[at_z(-step * d), h]
        pltpu.make_async_remote_copy(
            src_ref=slot, dst_ref=slot,
            send_sem=z_send.at[way, d - 1, h], recv_sem=z_recv.at[way, d - 1, h],
            device_id=(src_me, at_z(step)), device_id_type=MESH,
        ).wait_recv()

    def sibling(dz, h, wait=False):
        there = around(z, dz, NZ) * 2 + (1 - core if wait else core)
        slot = s_all.at[there, h]
        copy = pltpu.make_async_remote_copy(
            src_ref=slot, dst_ref=slot,
            send_sem=d_send.at[dz % NZ, h], recv_sem=d_recv.at[dz % NZ, h],
            device_id=(src_me, z * 2 + 1 - core), device_id_type=MESH,
        )
        if wait:
            copy.wait_recv()
        else:
            go(copy)

    def go(copy):
        copy.start()
        sent.append(copy)

    def z_event(d, h):
        for way in range(2):
            if d == NZ // 2 and h != way:
                continue
            z_landed(way, d, h)
            if d < NZ // 2 - 1 or (d == NZ // 2 - 1 and h == way):
                go(z_copy(way, d + 1, h))
            sibling(-d if way == 0 else d, h)

    def place(h, first, second):
        return at_xy(first, second) if h == 0 else at_xy(second, first)

    moves = ((1, 0), (-1, 0), (0, 1), (0, -1))

    def p_copy(h, index, slice_at, move):
        slot = t_all.at[place(h, *slice_at), h]
        go(pltpu.make_async_remote_copy(
            src_ref=slot, dst_ref=slot,
            send_sem=p_send.at[h, index], recv_sem=p_recv.at[h, index],
            device_id=(place(h, *moves[move]), tgt_me), device_id_type=MESH,
        ))

    def p_landed(h, index, slice_at):
        slot = t_all.at[place(h, *slice_at), h]
        pltpu.make_async_remote_copy(
            src_ref=slot, dst_ref=slot,
            send_sem=p_send.at[h, index], recv_sem=p_recv.at[h, index],
            device_id=(src_me, tgt_me), device_id_type=MESH,
        ).wait_recv()

    offsets = (0, -1, 1, 2)

    def p_second(h, j):
        p_copy(h, 3 + 3 * j, (offsets[j], 0), 2)
        p_copy(h, 4 + 3 * j, (offsets[j], 0), 3)

    def p_own():
        for h in range(2):
            p_copy(h, 0, (0, 0), 0)
            p_copy(h, 1, (0, 0), 1)
            p_second(h, 0)

    def p_first():
        for h in range(2):
            p_landed(h, 0, (-1, 0))
            p_copy(h, 2, (-1, 0), 0)
            p_second(h, 1)
        for h in range(2):
            p_landed(h, 1, (1, 0))
            p_second(h, 2)

    def p_opposite():
        for h in range(2):
            p_landed(h, 2, (-2, 0))
            p_second(h, 3)

    def p_lines(j):
        up = j in (0, 3)
        for h in range(2):
            p_landed(h, 3 + 3 * j, (offsets[j], -1))
            if up:
                p_copy(h, 5 + 3 * j, (offsets[j], -1), 2)
        for h in range(2):
            p_landed(h, 4 + 3 * j, (offsets[j], 1))
            if not up:
                p_copy(h, 5 + 3 * j, (offsets[j], 1), 3)

    def p_last():
        for j in range(4):
            for h in range(2):
                p_landed(h, 5 + 3 * j, (offsets[j], 2))

    for h in range(2):
        go(z_copy(0, 1, h))
        go(z_copy(1, 1, h))
    p_own()
    for h in range(2):
        sibling(0, h)
    p_first()
    z_event(1, 0)
    p_lines(0)
    z_event(1, 1)
    p_opposite()
    p_lines(1)
    z_event(2, 0)
    p_lines(2)
    z_event(2, 1)
    p_lines(3)
    z_event(3, 0)
    p_last()
    z_event(3, 1)
    z_event(4, 0)
    z_event(4, 1)
    for dz in range(NZ):
        for h in range(2):
            sibling(dz, h, wait=True)
    for copy in sent:
        copy.wait_send()

    depth = s_all.shape[0] * s_all.shape[1] * s_all.shape[2]
    tile = 256

    @pl.loop(0, sim.shape[0] // tile)
    def _(i):
        part = pl.ds(pl.multiple_of(i * tile, tile), tile)
        left = s_all[:, :, :, part].reshape(depth, tile)
        right = t_all[...].reshape(depth, sim.shape[1])
        sim[part, :] = lax.dot_general(
            left, right, (((0,), (0,)), ((), ())), preferred_element_type=F32
        )

    def sweep(change):
        @pl.loop(0, row_blocks)
        def _(b):
            def rows(g):
                return pl.ds(pl.multiple_of(b * LANES + g * 8, 8), 8)

            for g in range(16):
                beside = side[rows(g), :]
                values = []
                for c in range(col_blocks):
                    lane = pl.ds(c * LANES, LANES)
                    value = change(sim[rows(g), lane], beside, c)
                    sim[rows(g), lane] = value
                    values.append(value)
                best = merge4(sort4(values[:4]), sort4(values[4:]))
                for k in range(4):
                    lists[k, g * 8:(g + 1) * 8, :] = best[k]
            turned = [lists[k].T for k in range(4)]
            best = over_sublanes(tree([[t[g * 8:(g + 1) * 8] for t in turned] for g in range(16)]))
            for k in range(4):
                row_out[b, k:k + 1, :] = best[k][0:1]
            for c in range(col_blocks):
                lane = pl.ds(c * LANES, LANES)
                quads = [
                    sort4([sim[rows(4 * q + g), lane] for g in range(4)]) for q in range(4)
                ]
                best = merge4(tree(quads), [columns[c, k] for k in range(4)])
                for k in range(4):
                    columns[c, k] = best[k]

        for c in range(col_blocks):
            best = over_sublanes([columns[c, k] for k in range(4)])
            for k in range(4):
                col_out[c, k:k + 1, :] = best[k][0:1]

    axes = (
        (0, tgt_me, row_blocks, row_out, row_in, lambda v: (src_me, v)),
        (1, src_me, col_blocks, col_out, col_in, lambda v: (v, tgt_me)),
    )

    def exchange(stage, results, finish):
        def hand(a, me, blocks, out, into, device, r):
            to = around(me, r, GROUP)
            return pltpu.make_async_remote_copy(
                src_ref=out.at[lax.rem(to, blocks)], dst_ref=into.at[stage, me],
                send_sem=g_send.at[stage, a, r], recv_sem=g_recv.at[stage, a, r],
                device_id=device(to), device_id_type=MESH,
            ), to

        def share(a, me, result, device, r):
            return pltpu.make_async_remote_copy(
                src_ref=result.at[me], dst_ref=result.at[me],
                send_sem=h_send.at[stage, a, r], recv_sem=h_recv.at[stage, a, me],
                device_id=device(around(me, r, GROUP)), device_id_type=MESH,
            )

        for a, me, blocks, out, into, device in axes:
            for r in range(1, GROUP):
                copy, to = hand(a, me, blocks, out, into, device, r)

                @pl.when(to < blocks)
                def _(copy=copy):
                    copy.start()

        for (a, me, blocks, out, into, device), result in zip(axes, results):
            @pl.when(me < blocks)
            def _(a=a, me=me, blocks=blocks, out=out, into=into, device=device, result=result):
                into[stage, me] = out[me]
                for r in range(1, GROUP):
                    pltpu.make_async_remote_copy(
                        src_ref=out.at[0], dst_ref=into.at[stage, around(me, -r, GROUP)],
                        send_sem=g_send.at[stage, a, r], recv_sem=g_recv.at[stage, a, r],
                        device_id=device(me), device_id_type=MESH,
                    ).wait_recv()
                halves = [[into[stage, pl.ds(p, 8), k, :] for k in range(4)] for p in (0, 8)]
                finish(result, me, over_sublanes(merge4(*halves)))
                for r in range(1, GROUP):
                    share(a, me, result, device, r).start()

        for (a, me, blocks, out, into, device), result in zip(axes, results):
            for b in range(blocks):
                @pl.when(me != b)
                def _(b=b, a=a, device=device, result=result, me=me):
                    pltpu.make_async_remote_copy(
                        src_ref=result.at[b], dst_ref=result.at[b],
                        send_sem=h_send.at[stage, a, 0], recv_sem=h_recv.at[stage, a, b],
                        device_id=device(me), device_id_type=MESH,
                    ).wait_recv()

        for (a, me, blocks, out, into, device), result in zip(axes, results):
            for r in range(1, GROUP):
                copy, to = hand(a, me, blocks, out, into, device, r)

                @pl.when(to < blocks)
                def _(copy=copy):
                    copy.wait_send()

            @pl.when(me < blocks)
            def _(a=a, me=me, device=device, result=result):
                for r in range(1, GROUP):
                    share(a, me, result, device, r).wait_send()

    def scaled(value, beside, c):
        return value * beside * tgt_scale[:, c * LANES:(c + 1) * LANES]

    def half_mean(result, me, best):
        result[me] = (best[0] + best[1] + best[2] + best[3]) * 0.125

    sweep(scaled)
    exchange(0, (row_mean, col_mean), half_mean)

    for b in range(row_blocks):
        line = row_mean[b]
        side[b * LANES:(b + 1) * LANES, :] = jnp.concatenate([line] * 16, axis=0).T
    columns[...] = jnp.full(columns.shape, LOW, F32)

    def margin(value, beside, c):
        return value / (beside + col_mean[c])

    def keep(result, me, best):
        for k in range(4):
            result[me, k:k + 1, :] = best[k][0:1]

    sweep(margin)
    exchange(1, (row_best, col_best), keep)

    for b in range(row_blocks):
        fwd_ref[:, b * LANES:(b + 1) * LANES] = row_best[b, 0:4, :]
    for c in range(col_blocks):
        bwd_ref[:, c * LANES:(c + 1) * LANES] = col_best[c, 0:4, :]


def body(src_codes, src_scale, tgt_codes, tgt_scale):
    depth, rows = src_codes.shape
    cols = tgt_codes.shape[1]
    row_blocks, col_blocks = rows // LANES, cols // LANES
    vmem = pl.BlockSpec(memory_space=pltpu.VMEM)
    hbm = pl.BlockSpec(memory_space=pl.ANY)
    dma = pltpu.SemaphoreType.DMA
    return pl.pallas_call(
        kernel,
        out_shape=(
            jax.ShapeDtypeStruct((4, rows), F32),
            jax.ShapeDtypeStruct((4, cols), F32),
        ),
        in_specs=[hbm, vmem, hbm, vmem],
        out_specs=(vmem, vmem),
        scratch_shapes=[
            pltpu.VMEM((GROUP, 2, depth // 2, rows), jnp.bfloat16),
            pltpu.VMEM((GROUP, 2, depth // 2, cols), jnp.bfloat16),
            pltpu.VMEM((rows, cols), F32),
            pltpu.VMEM((rows, LANES), F32),
            pltpu.VMEM((4, LANES, LANES), F32),
            pltpu.VMEM((col_blocks, 4, 8, LANES), F32),
            pltpu.VMEM((row_blocks, 8, LANES), F32),
            pltpu.VMEM((2, GROUP, 8, LANES), F32),
            pltpu.VMEM((row_blocks, 8, LANES), F32),
            pltpu.VMEM((row_blocks, 8, LANES), F32),
            pltpu.VMEM((col_blocks, 8, LANES), F32),
            pltpu.VMEM((2, GROUP, 8, LANES), F32),
            pltpu.VMEM((col_blocks, 8, LANES), F32),
            pltpu.VMEM((col_blocks, 8, LANES), F32),
            dma((2, 2)),
            dma((2, NZ // 2, 2)),
            dma((2, NZ // 2, 2)),
            dma((NZ, 2)),
            dma((NZ, 2)),
            dma((2, 15)),
            dma((2, 15)),
            dma((2, 2, GROUP)),
            dma((2, 2, GROUP)),
            dma((2, 2, GROUP)),
            dma((2, 2, GROUP)),
        ],
        compiler_params=pltpu.CompilerParams(
            collective_id=0, has_side_effects=True, vmem_limit_bytes=40 * 1024 * 1024
        ),
        name="mine",
    )(src_codes, src_scale.reshape(1, rows), tgt_codes, tgt_scale.reshape(1, cols))


def solution(mesh):
    placed = (P("tgt", "src"), P("src"), P("src", "tgt"), P("tgt"))
    return jax.shard_map(
        body,
        mesh=mesh,
        in_specs=placed,
        out_specs=(P(None, "src"), P(None, "tgt")),
        check_vma=False,
    )
```

time: 376 us -> 72.7 us (0.19)
  waiting for transfers between devices: 99.6 us -> 0 us
  blocking collectives: 79.3 us -> 0 us
  other arithmetic: 71.2 us -> 0 us
  Pallas kernels: 0 us -> 68.1 us
  matrix products: 52.9 us -> 0 us
  local copies, waits for them, and re-layouts: 34 us -> 3.76 us
  loops' own time: 23.3 us -> 0 us
  between operations: 14.2 us -> 0.65 us
    all_gather x2 -> x0, waiting for transfers between devices: 98.2 us -> none  [the longest x1 54.7 us: body(): targets = lax.all_gather(tgt_codes, 'src', axis=0, tiled=True)]
    all_gather x4 -> x0, blocking collectives: 79.3 us -> none  [combined_all(): gathered = jax.tree.map(lambda a: lax.all_gather(a, axis), part)]
    pallas_call x0 -> x1, Pallas kernels: none -> 68.1 us  [body(): pl.pallas_call(kernel, out_shape=(jax.ShapeDtypeStruct((4, rows), F32), j...]
    dot_general x24 -> x0, matrix products: 52.9 us -> none  [tile_scores(): lax.dot_general(block, targets, (((0,), (0,)), ((), ())), preferred_eleme...]
    reduce_max x600 -> x0, other arithmetic: 35.5 us -> none  [best_values(): largest = jnp.max(values, axis=axis, keepdims=True)]
    reduce_min x348 -> x0, other arithmetic: 33 us -> none  [best_values(): jnp.min(jnp.where(values == largest, places, length), axis=axis, keepdims...]
    another operation x6 -> x0, loops' own time: 23.3 us -> none  [the longest x2 17.1 us: sweep(): behind, ahead = lax.scan(visit, start, items)]
    mul x24 -> x0, local copies, waits for them, and re-layouts: 16.8 us -> none  [tile_scores(): return dots * block_scale[:, None] * target_scale[None, :]]
  transfers between devices with their start and end apart: 2 -> 0, of which waited for: 2 -> 0; matrix products, arithmetic and copies ran while one was open for 0% -> 0% of each run, Pallas kernels for 0% -> 0%
where the time goes in v1:
time: 72.7 us; the launch traced here: 72.6 us
  Pallas kernels  68.1 us (94%)
  local copies, waits for them, and re-layouts  3.76 us (5%)
    pallas_call x1, Pallas kernels, body(): pl.pallas_call(kernel, out_shape=(jax.ShapeDtypeStruct((4, rows), F32), j...  68.1 us
    unnamed x8, local copies, waits for them, and re-layouts  3.05 us

profile of v1, /device:TPU:1, one launch (start us, length us, event | category | flops | bytes accessed | tf_op | source)
XLA Modules:
  0.0 72.6 jit_solution(8959328103156682363)
XLA Ops:
  0.6 0.0 copy-start.2
  0.6 0.7 reshape.10.src_scale
  1.3 0.0 copy-done.2
  1.4 0.0 copy-start
  1.4 0.9 %copy-done = bf16[64,1536]{1,0:T(8,128)(2,1)S(1)} copy-done((bf16[64,1536]{1,0:T(8,128)(2,1)S(1)}, bf16[64,1536]{1,0:T(8,128)(2,1)}, u32[]{:S(2)}) %copy-start) | copy-done | bytes 196632
  2.3 0.0 copy-start.1
  2.3 0.9 %copy-done.1 = bf16[64,1024]{1,0:T(8,128)(2,1)S(1)} copy-done((bf16[64,1024]{1,0:T(8,128)(2,1)S(1)}, bf16[64,1024]{1,0:T(8,128)(2,1)}, u32[]{:S(2)}) %copy-start.1) | copy-done | bytes 131096
  3.2 68.1 %mine.1 = (f32[4,1536]{1,0:T(4,128)S(1)}, f32[4,1024]{1,0:T(4,128)S(1)}) custom-call(bf16[64,1536]{1,0:T(8,128)(2,1)S(1)} %copy-done, f32[1,1536]{1,0:T(1,128)S(1)} %reshape.10.src_scale, bf16[64,1024]{1,0:T(8,128)(2,1)S(1)} %copy-done.1, f32[1,1024]{1,0:T(1,128)S(1)} %bitcast.1), custom_call_target="tpu_custom_call" | custom-call | tf_op jit(solution)/shard_map/mine/pallas_call | solution.py:387
  71.3 0.6 copy.8
  72.0 0.6 copy.9
Async XLA Ops:
  0.6 0.7 copy-start.2
  1.4 0.9 %copy-start = (bf16[64,1536]{1,0:T(8,128)(2,1)S(1)}, bf16[64,1536]{1,0:T(8,128)(2,1)}, u32[]{:S(2)}) copy-start(bf16[64,1536]{1,0:T(8,128)(2,1)} %src_ref.1) | copy-start | bytes 589828
  2.3 0.9 %copy-start.1 = (bf16[64,1024]{1,0:T(8,128)(2,1)S(1)}, bf16[64,1024]{1,0:T(8,128)(2,1)}, u32[]{:S(2)}) copy-start(bf16[64,1024]{1,0:T(8,128)(2,1)} %tgt_ref.1) | copy-start | bytes 393220

commit v2 on v1

v2 whole, which is shorter than its diff:
```python
import jax
import jax.numpy as jnp
from jax import lax
from jax.experimental import pallas as pl
from jax.experimental.pallas import tpu as pltpu
from jax.sharding import PartitionSpec as P

MESH = pl.DeviceIdType.MESH
F32 = jnp.float32
LOW = -1e30

NX, NY, NZ = 4, 4, 8
GROUP = 16
LANES = 128
PIECES = 4
TILE = 256


def compare(a, b):
    return jnp.maximum(a, b), jnp.minimum(a, b)


def sort4(v):
    a, b = compare(v[0], v[1])
    c, d = compare(v[2], v[3])
    a, c = compare(a, c)
    b, d = compare(b, d)
    b, c = compare(b, c)
    return [a, b, c, d]


def merge4(p, q):
    a, b, c, d = [jnp.maximum(p[i], q[3 - i]) for i in range(4)]
    a, c = compare(a, c)
    b, d = compare(b, d)
    a, b = compare(a, b)
    c, d = compare(c, d)
    return [a, b, c, d]


def tree(lists):
    while len(lists) > 1:
        odd = lists[len(lists) // 2 * 2:]
        lists = [merge4(lists[i], lists[i + 1]) for i in range(0, len(lists) - 1, 2)] + odd
    return lists[0]


def over_sublanes(best):
    for shift in (4, 2, 1):
        best = merge4(best, [pltpu.roll(v, shift, 0) for v in best])
    return best


TAIL = (32, 40, 44, 36)


def row_line(k, b):
    return jnp.where(b < 8, 8 * k + b, TAIL[k] + b - 8)


def load_rows(ref):
    head = [ref[8 * k:8 * k + 8, :] for k in range(4)]
    first, second = ref[32:40, :], ref[40:48, :]
    return head, [first, second, pltpu.roll(second, 4, 0), pltpu.roll(first, 4, 0)]


def kernel(
    src_ref, src_scale, tgt_ref, tgt_scale, fwd_ref, bwd_ref,
    s_all, t_all, sim, side, lists, columns,
    row_out, row_in, pair_out, pair_in,
    col_out, col_in, col_mean,
    own_sem, z_send, z_recv, d_send, d_recv, p_send, p_recv, p_rest,
    x_send, x_recv,
):
    src_me, tgt_me = lax.axis_index("src"), lax.axis_index("tgt")
    x, y = src_me // NY, lax.rem(src_me, NY)
    z, core = tgt_me // 2, lax.rem(tgt_me, 2)
    row_blocks, col_blocks = sim.shape[0] // LANES, sim.shape[1] // LANES

    def around(v, step, n):
        return lax.rem(v + (step + n), n)

    def at_xy(dx, dy):
        return around(x, dx, NX) * NY + around(y, dy, NY)

    def at_z(dz):
        return around(z, dz, NZ) * 2 + core

    twin = (src_me, z * 2 + 1 - core)

    barrier = pltpu.get_barrier_semaphore()
    neighbours = [(src_me, at_z(1)), (src_me, at_z(-1)), twin]
    neighbours += [(at_xy(*move), tgt_me) for move in ((1, 0), (-1, 0), (0, 1), (0, -1))]
    for device in neighbours:
        pl.semaphore_signal(barrier, inc=1, device_id=device, device_id_type=MESH)

    own = []
    for h in range(PIECES):
        part = pl.ds(h * 16, 16)
        own.append(pltpu.make_async_copy(src_ref.at[part], s_all.at[tgt_me, h], own_sem.at[0, h]))
    for h in range(2):
        part = pl.ds(h * 32, 32)
        own.append(pltpu.make_async_copy(tgt_ref.at[part], t_all.at[src_me, h], own_sem.at[1, h]))
    for copy in own:
        copy.start()

    for copy in own:
        copy.wait()
    pl.semaphore_wait(barrier, len(neighbours))

    def z_copy(way, d, h, landed=False):
        step = 1 if way == 0 else -1
        slot = s_all.at[at_z(-step * (d if landed else d - 1)), h]
        return pltpu.make_async_remote_copy(
            src_ref=slot, dst_ref=slot,
            send_sem=z_send, recv_sem=z_recv.at[way, d - 1, h],
            device_id=(src_me, at_z(step)), device_id_type=MESH,
        )

    def goes(way, d, h):
        return d < NZ // 2 or (d == NZ // 2 and (h < PIECES // 2) == (way == 0))

    def to_twin(dz, h):
        slot = s_all.at[at_z(dz), h]
        pltpu.make_async_remote_copy(
            src_ref=slot, dst_ref=slot, send_sem=d_send, recv_sem=d_recv.at[dz % NZ],
            device_id=twin, device_id_type=MESH,
        ).start()

    def from_twin(dz):
        slot = s_all.at[around(z, dz, NZ) * 2 + 1 - core]
        pltpu.make_async_remote_copy(
            src_ref=slot, dst_ref=slot, send_sem=d_send, recv_sem=d_recv.at[dz % NZ],
            device_id=twin, device_id_type=MESH,
        ).wait_recv()

    def z_event(d, h):
        for way in range(2):
            if goes(way, d, h):
                z_copy(way, d, h, landed=True).wait_recv()
                if goes(way, d + 1, h):
                    z_copy(way, d + 1, h).start()
                to_twin(-d if way == 0 else d, h)

    def place(h, first, second):
        return at_xy(first, second) if h == 0 else at_xy(second, first)

    moves = ((1, 0), (-1, 0), (0, 1), (0, -1))

    def p_copy(h, index, slice_at, move):
        slot = t_all.at[place(h, *slice_at), h]
        return pltpu.make_async_remote_copy(
            src_ref=slot, dst_ref=slot,
            send_sem=p_send, recv_sem=p_rest if index is None else p_recv.at[h, index],
            device_id=(place(h, *moves[move]), tgt_me), device_id_type=MESH,
        )

    offsets = (0, -1, 1, 2)
    upward = (True, False, False, True)

    def p_second(h, j):
        p_copy(h, 3 + j if upward[j] else None, (offsets[j], 0), 2).start()
        p_copy(h, None if upward[j] else 3 + j, (offsets[j], 0), 3).start()

    def p_own():
        for h in range(2):
            p_copy(h, 0, (0, 0), 0).start()
            p_copy(h, 1, (0, 0), 1).start()
            p_second(h, 0)

    def p_first():
        for h in range(2):
            p_copy(h, 0, (-1, 0), 0).wait_recv()
            p_copy(h, 2, (-1, 0), 0).start()
            p_second(h, 1)
        for h in range(2):
            p_copy(h, 1, (1, 0), 0).wait_recv()
            p_second(h, 2)

    def p_opposite():
        for h in range(2):
            p_copy(h, 2, (-2, 0), 0).wait_recv()
            p_second(h, 3)

    def p_line(j):
        for h in range(2):
            slice_at = (offsets[j], -1 if upward[j] else 1)
            p_copy(h, 3 + j, slice_at, 2).wait_recv()
            p_copy(h, None, slice_at, 2 if upward[j] else 3).start()

    for h in range(PIECES):
        for way in range(2):
            z_copy(way, 1, h).start()
    p_own()
    for h in range(PIECES):
        to_twin(0, h)

    for b in range(row_blocks):
        line = src_scale[:, b * LANES:(b + 1) * LANES]
        side[b * LANES:(b + 1) * LANES, :] = jnp.broadcast_to(line, (LANES, LANES)).T
    columns[...] = jnp.full(columns.shape, LOW, F32)

    p_first()
    z_event(1, 0)
    p_line(0)
    z_event(1, 1)
    p_opposite()
    z_event(1, 2)
    p_line(1)
    z_event(1, 3)
    z_event(2, 0)
    p_line(2)
    z_event(2, 1)
    p_line(3)
    z_event(2, 2)
    z_event(2, 3)
    pltpu.make_async_copy(t_all.at[pl.ds(0, 8)], t_all.at[pl.ds(0, 8)], p_rest).wait()

    def features(dz, part):
        return s_all[pl.ds(around(z, dz, NZ) * 2, 2), :, :, part].reshape(LANES, TILE)

    def targets(dz):
        return t_all[pl.ds(around(z, dz, NZ) * 2, 2)].reshape(LANES, sim.shape[1])

    def product(first, second, start, stop, fresh=False):
        @pl.loop(start, stop)
        def _(i):
            part = pl.ds(pl.multiple_of(i * TILE, TILE), TILE)
            left = jnp.concatenate([features(first, part), features(second, part)], axis=0)
            right = jnp.concatenate([targets(first), targets(second)], axis=0)
            dots = lax.dot_general(
                left, right, (((0,), (0,)), ((), ())), preferred_element_type=F32
            )
            if fresh:
                sim[part, :] = dots
            else:
                sim[part, :] = sim[part, :] + dots

    tiles = sim.shape[0] // TILE
    half = tiles // 2
    from_twin(-1)
    from_twin(1)
    z_event(3, 0)
    product(-1, 1, 0, half, fresh=True)
    z_event(3, 1)
    product(-1, 1, half, tiles, fresh=True)
    from_twin(-2)
    from_twin(2)
    z_event(3, 2)
    product(-2, 2, 0, half)
    z_event(3, 3)
    product(-2, 2, half, tiles)
    from_twin(-3)
    from_twin(3)
    z_event(4, 0)
    z_event(4, 2)
    product(-3, 3, 0, half)
    z_event(4, 1)
    z_event(4, 3)
    product(-3, 3, half, tiles)
    from_twin(0)
    from_twin(4)
    product(0, 4, 0, tiles)

    for slots, sem in ((s_all.at[pl.ds(0, 7)], z_send), (s_all.at[pl.ds(0, 8)], d_send),
                       (t_all.at[pl.ds(0, 15)], p_send)):
        pltpu.make_async_copy(slots, slots, sem).wait()

    def sweep(change):
        @pl.loop(0, row_blocks)
        def _(b):
            def rows(g):
                return pl.ds(pl.multiple_of(b * LANES + g * 8, 8), 8)

            for g in range(16):
                beside = side[rows(g), :]
                values = []
                for c in range(col_blocks):
                    lane = pl.ds(c * LANES, LANES)
                    value = change(sim[rows(g), lane], beside, c)
                    sim[rows(g), lane] = value
                    values.append(value)
                best = merge4(sort4(values[:4]), sort4(values[4:]))
                for k in range(4):
                    lists[k, g * 8:(g + 1) * 8, :] = best[k]
            turned = [lists[k].T for k in range(4)]
            best = over_sublanes(tree([[t[g * 8:(g + 1) * 8] for t in turned] for g in range(16)]))
            for k in range(4):
                row_out[pl.ds(row_line(k, b), 1), :] = best[k][0:1]
            for c in range(col_blocks):
                lane = pl.ds(c * LANES, LANES)
                quads = [
                    sort4([sim[rows(4 * q + g), lane] for g in range(4)]) for q in range(4)
                ]
                best = merge4(tree(quads), [columns[c, k] for k in range(4)])
                for k in range(4):
                    columns[c, k] = best[k]

        for c in range(col_blocks):
            best = over_sublanes([columns[c, k] for k in range(4)])
            for k in range(4):
                col_out[k, c:c + 1, :] = best[k][0:1]

    def exchange(stage):
        sends = []
        for r in range(1, NZ):
            sends.append(pltpu.make_async_remote_copy(
                src_ref=row_out, dst_ref=row_in.at[stage, r - 1],
                send_sem=x_send.at[0], recv_sem=x_recv.at[stage, 0],
                device_id=(src_me, at_z(r)), device_id_type=MESH,
            ))
        for r in range(1, GROUP):
            sends.append(pltpu.make_async_remote_copy(
                src_ref=col_out, dst_ref=col_in.at[stage, r - 1],
                send_sem=x_send.at[1], recv_sem=x_recv.at[stage, 1],
                device_id=(around(src_me, r, GROUP), tgt_me), device_id_type=MESH,
            ))
        for copy in sends:
            copy.start()
        row_slots, col_slots = row_in.at[stage], col_in.at[stage]

        pltpu.make_async_copy(row_slots, row_slots, x_recv.at[stage, 0]).wait()
        ours = [load_rows(row_out)] + [load_rows(row_in.at[stage, r]) for r in range(NZ - 1)]
        head, tail = tree([v[0] for v in ours]), tree([v[1] for v in ours])
        for k in range(4):
            pair_out[8 * k:8 * k + 8, :] = head[k]
            pair_out[TAIL[k]:TAIL[k] + 4, :] = tail[k][0:4]
        pair = pltpu.make_async_remote_copy(
            src_ref=pair_out, dst_ref=pair_in.at[stage],
            send_sem=x_send.at[2], recv_sem=x_recv.at[stage, 2],
            device_id=twin, device_id_type=MESH,
        )
        pair.start()

        pltpu.make_async_copy(col_slots, col_slots, x_recv.at[stage, 1]).wait()
        everyone = [[col_out[k] for k in range(4)]]
        everyone += [[col_in[stage, r, k] for k in range(4)] for r in range(GROUP - 1)]
        col_best = tree(everyone)

        pair.wait_recv()
        other_head, other_tail = load_rows(pair_in.at[stage])
        head, tail = merge4(head, other_head), merge4(tail, other_tail)
        pair.wait_send()
        pltpu.make_async_copy(row_slots, row_slots, x_send.at[0]).wait()
        pltpu.make_async_copy(col_slots, col_slots, x_send.at[1]).wait()
        return head, tail, col_best

    def line_of(head, tail, b):
        return head[b:b + 1] if b < 8 else tail[b - 8:b - 7]

    def scaled(value, beside, c):
        return value * beside * tgt_scale[:, c * LANES:(c + 1) * LANES]

    def half_mean(best):
        return (best[0] + best[1] + best[2] + best[3]) * 0.125

    sweep(scaled)
    head, tail, col_best = exchange(0)

    head, tail, beneath = half_mean(head), half_mean(tail), half_mean(col_best)
    for b in range(row_blocks):
        line = line_of(head, tail, b)
        side[b * LANES:(b + 1) * LANES, :] = jnp.broadcast_to(line, (LANES, LANES)).T
    for c in range(col_blocks):
        col_mean[c] = jnp.broadcast_to(beneath[c:c + 1], (8, LANES))
    columns[...] = jnp.full(columns.shape, LOW, F32)

    def margin(value, beside, c):
        return value / (beside + col_mean[c])

    sweep(margin)
    head, tail, col_best = exchange(1)
    for k in range(4):
        for b in range(row_blocks):
            fwd_ref[k:k + 1, b * LANES:(b + 1) * LANES] = line_of(head[k], tail[k], b)
        for c in range(col_blocks):
            bwd_ref[k:k + 1, c * LANES:(c + 1) * LANES] = col_best[k][c:c + 1]


def body(src_codes, src_scale, tgt_codes, tgt_scale):
    depth, rows = src_codes.shape
    cols = tgt_codes.shape[1]
    col_blocks = cols // LANES
    vmem = pl.BlockSpec(memory_space=pltpu.VMEM)
    hbm = pl.BlockSpec(memory_space=pltpu.HBM)
    dma = pltpu.SemaphoreType.DMA
    return pl.pallas_call(
        kernel,
        out_shape=(
            jax.ShapeDtypeStruct((4, rows), F32),
            jax.ShapeDtypeStruct((4, cols), F32),
        ),
        in_specs=[hbm, vmem, hbm, vmem],
        out_specs=(vmem, vmem),
        scratch_shapes=[
            pltpu.VMEM((GROUP, PIECES, depth // PIECES, rows), jnp.bfloat16),
            pltpu.VMEM((GROUP, 2, depth // 2, cols), jnp.bfloat16),
            pltpu.VMEM((rows, cols), F32),
            pltpu.VMEM((rows, LANES), F32),
            pltpu.VMEM((4, LANES, LANES), F32),
            pltpu.VMEM((col_blocks, 4, 8, LANES), F32),
            pltpu.VMEM((48, LANES), F32),
            pltpu.VMEM((2, NZ - 1, 48, LANES), F32),
            pltpu.VMEM((48, LANES), F32),
            pltpu.VMEM((2, 48, LANES), F32),
            pltpu.VMEM((4, 8, LANES), F32),
            pltpu.VMEM((2, GROUP - 1, 4, 8, LANES), F32),
            pltpu.VMEM((col_blocks, 8, LANES), F32),
            dma((2, 4)),
            dma,
            dma((2, NZ // 2, PIECES)),
            dma,
            dma((NZ,)),
            dma,
            dma((2, 7)),
            dma,
            dma((3,)),
            dma((2, 3)),
        ],
        compiler_params=pltpu.CompilerParams(
            collective_id=0, has_side_effects=True, vmem_limit_bytes=40 * 1024 * 1024
        ),
        name="mine",
    )(src_codes, src_scale.reshape(1, rows), tgt_codes, tgt_scale.reshape(1, cols))


def solution(mesh):
    placed = (P("tgt", "src"), P("src"), P("src", "tgt"), P("tgt"))
    return jax.shard_map(
        body,
        mesh=mesh,
        in_specs=placed,
        out_specs=(P(None, "src"), P(None, "tgt")),
        check_vma=False,
    )
```

time: 72.7 us -> 64.9 us (0.89)
  Pallas kernels: 68.1 us -> 60.3 us
    pallas_call x1, Pallas kernels: 68.1 us -> 60.3 us  [body(): pl.pallas_call(kernel, out_shape=(jax.ShapeDtypeStruct((4, rows), F32), j...]
where the time goes in v2:
time: 64.9 us; the launch traced here: 64.7 us
  Pallas kernels  60.3 us (93%)
  local copies, waits for them, and re-layouts  3.76 us (6%)
  between operations  0.65 us (1%)
    pallas_call x1, Pallas kernels, body(): pl.pallas_call(kernel, out_shape=(jax.ShapeDtypeStruct((4, rows), F32), j...  60.3 us
    unnamed x8, local copies, waits for them, and re-layouts  3.05 us

profile of v2, /device:TPU:1, one launch (start us, length us, event | category | flops | bytes accessed | tf_op | source)
XLA Modules:
  0.0 64.7 jit_solution(6056127274084368918)
XLA Ops:
  0.6 0.0 copy-start.2
  0.6 0.7 %reshape.10.src_scale = f32[1,1536]{1,0:T(1,128)S(1)} reshape(f32[1536]{0:T(1024)} %param.5) | data formatting | bytes 12288 | tf_op jit(solution)/shard_map/reshape | solution.py:424
  1.3 0.0 copy-done.2
  1.4 0.0 copy-start
  1.4 0.9 %copy-done = bf16[64,1536]{1,0:T(8,128)(2,1)S(1)} copy-done((bf16[64,1536]{1,0:T(8,128)(2,1)S(1)}, bf16[64,1536]{1,0:T(8,128)(2,1)}, u32[]{:S(2)}) %copy-start) | copy-done | bytes 196632
  2.3 0.0 copy-start.1
  2.3 0.9 %copy-done.1 = bf16[64,1024]{1,0:T(8,128)(2,1)S(1)} copy-done((bf16[64,1024]{1,0:T(8,128)(2,1)S(1)}, bf16[64,1024]{1,0:T(8,128)(2,1)}, u32[]{:S(2)}) %copy-start.1) | copy-done | bytes 131096
  3.2 60.3 %mine.1 = (f32[4,1536]{1,0:T(4,128)S(1)}, f32[4,1024]{1,0:T(4,128)S(1)}) custom-call(bf16[64,1536]{1,0:T(8,128)(2,1)S(1)} %copy-done, f32[1,1536]{1,0:T(1,128)S(1)} %reshape.10.src_scale, bf16[64,1024]{1,0:T(8,128)(2,1)S(1)} %copy-done.1, f32[1,1024]{1,0:T(1,128)S(1)} %bitcast.1), custom_call_target="tpu_custom_call" | custom-call | tf_op jit(solution)/shard_map/mine/pallas_call | solution.py:387
  63.5 0.6 copy.8
  64.1 0.6 copy.9
Async XLA Ops:
  0.6 0.7 %copy-start.2 = (f32[1024]{0:T(1024)S(1)}, f32[1024]{0:T(1024)}, u32[]{:S(2)}) copy-start(f32[1024]{0:T(1024)} %param.7) | copy-start | bytes 12292
  1.4 0.9 %copy-start = (bf16[64,1536]{1,0:T(8,128)(2,1)S(1)}, bf16[64,1536]{1,0:T(8,128)(2,1)}, u32[]{:S(2)}) copy-start(bf16[64,1536]{1,0:T(8,128)(2,1)} %src_ref.1) | copy-start | bytes 589828
  2.3 0.9 %copy-start.1 = (bf16[64,1024]{1,0:T(8,128)(2,1)S(1)}, bf16[64,1024]{1,0:T(8,128)(2,1)}, u32[]{:S(2)}) copy-start(bf16[64,1024]{1,0:T(8,128)(2,1)} %tgt_ref.1) | copy-start | bytes 393220

commit v3 on v2

--- a/solution.py
+++ b/solution.py
@@ -13,7 +13,8 @@
 GROUP = 16
 LANES = 128
 PIECES = 4
-TILE = 256
+QUARTERS = 4
+TILE = 1536
 
 
 def compare(a, b):
@@ -90,7 +91,8 @@
 
     barrier = pltpu.get_barrier_semaphore()
     neighbours = [(src_me, at_z(1)), (src_me, at_z(-1)), twin]
-    neighbours += [(at_xy(*move), tgt_me) for move in ((1, 0), (-1, 0), (0, 1), (0, -1))]
+    steps = ((1, 0), (-1, 0), (2, 0), (0, 1), (0, -1), (0, 2))
+    neighbours += [(at_xy(*step), tgt_me) for step in steps]
     for device in neighbours:
         pl.semaphore_signal(barrier, inc=1, device_id=device, device_id_type=MESH)
 
@@ -98,8 +100,8 @@
     for h in range(PIECES):
         part = pl.ds(h * 16, 16)
         own.append(pltpu.make_async_copy(src_ref.at[part], s_all.at[tgt_me, h], own_sem.at[0, h]))
-    for h in range(2):
-        part = pl.ds(h * 32, 32)
+    for h in range(QUARTERS):
+        part = pl.ds(h * 16, 16)
         own.append(pltpu.make_async_copy(tgt_ref.at[part], t_all.at[src_me, h], own_sem.at[1, h]))
     for copy in own:
         copy.start()
@@ -117,8 +119,11 @@
             device_id=(src_me, at_z(step)), device_id_type=MESH,
         )
 
-    def goes(way, d, h):
-        return d < NZ // 2 or (d == NZ // 2 and (h < PIECES // 2) == (way == 0))
+    def piece(way, i):
+        return (i + way * PIECES // 2) % PIECES
+
+    def goes(d, i):
+        return d < NZ // 2 or (d == NZ // 2 and i < PIECES // 2)
 
     def to_twin(dz, h):
         slot = s_all.at[at_z(dz), h]
@@ -134,86 +139,105 @@
             device_id=twin, device_id_type=MESH,
         ).wait_recv()
 
-    def z_event(d, h):
+    def z_event(d, i):
         for way in range(2):
-            if goes(way, d, h):
+            if goes(d, i):
+                h = piece(way, i)
                 z_copy(way, d, h, landed=True).wait_recv()
-                if goes(way, d + 1, h):
+                if goes(d + 1, i):
                     z_copy(way, d + 1, h).start()
                 to_twin(-d if way == 0 else d, h)
 
     def place(h, first, second):
-        return at_xy(first, second) if h == 0 else at_xy(second, first)
-
-    moves = ((1, 0), (-1, 0), (0, 1), (0, -1))
+        return at_xy(first, second) if h % 2 == 0 else at_xy(second, first)
 
     def p_copy(h, index, slice_at, move):
         slot = t_all.at[place(h, *slice_at), h]
         return pltpu.make_async_remote_copy(
             src_ref=slot, dst_ref=slot,
             send_sem=p_send, recv_sem=p_rest if index is None else p_recv.at[h, index],
-            device_id=(place(h, *moves[move]), tgt_me), device_id_type=MESH,
+            device_id=(place(h, *move), tgt_me), device_id_type=MESH,
         )
 
+    up, down = (0, 1), (0, -1)
     offsets = (0, -1, 1, 2)
-    upward = (True, False, False, True)
-
-    def p_second(h, j):
-        p_copy(h, 3 + j if upward[j] else None, (offsets[j], 0), 2).start()
-        p_copy(h, None if upward[j] else 3 + j, (offsets[j], 0), 3).start()
-
-    def p_own():
-        for h in range(2):
-            p_copy(h, 0, (0, 0), 0).start()
-            p_copy(h, 1, (0, 0), 1).start()
-            p_second(h, 0)
-
-    def p_first():
-        for h in range(2):
-            p_copy(h, 0, (-1, 0), 0).wait_recv()
-            p_copy(h, 2, (-1, 0), 0).start()
-            p_second(h, 1)
-        for h in range(2):
-            p_copy(h, 1, (1, 0), 0).wait_recv()
-            p_second(h, 2)
-
-    def p_opposite():
-        for h in range(2):
-            p_copy(h, 2, (-2, 0), 0).wait_recv()
-            p_second(h, 3)
-
-    def p_line(j):
-        for h in range(2):
-            slice_at = (offsets[j], -1 if upward[j] else 1)
-            p_copy(h, 3 + j, slice_at, 2).wait_recv()
-            p_copy(h, None, slice_at, 2 if upward[j] else 3).start()
-
-    for h in range(PIECES):
+    upward = (True, False, False, False)
+
+    def second(h, j):
+        p_copy(h, 3 + j if upward[j] else None, (offsets[j], 0), up).start()
+        p_copy(h, None if upward[j] else 3 + j, (offsets[j], 0), down).start()
+
+    def below(h):
+        p_copy(h, 0, (-1, 0), up).wait_recv()
+        second(h, 1)
+
+    def above(h):
+        p_copy(h, 1, (1, 0), up).wait_recv()
+        second(h, 2)
+
+    def across(h):
+        p_copy(h, 2, (2, 0), up).wait_recv()
+        second(h, 3)
+
+    def line(h, j):
+        slice_at = (offsets[j], -1 if upward[j] else 1)
+        p_copy(h, 3 + j, slice_at, up).wait_recv()
+        p_copy(h, None, slice_at, up if upward[j] else down).start()
+
+    for i in range(PIECES):
         for way in range(2):
-            z_copy(way, 1, h).start()
-    p_own()
+            z_copy(way, 1, piece(way, i)).start()
+    for h in range(QUARTERS):
+        p_copy(h, 0, (0, 0), (1, 0)).start()
+        p_copy(h, 1, (0, 0), (-1, 0)).start()
+        p_copy(h, 2, (0, 0), (2, 0)).start()
+    for h in range(QUARTERS):
+        second(h, 0)
     for h in range(PIECES):
         to_twin(0, h)
 
     for b in range(row_blocks):
-        line = src_scale[:, b * LANES:(b + 1) * LANES]
-        side[b * LANES:(b + 1) * LANES, :] = jnp.broadcast_to(line, (LANES, LANES)).T
+        scales = src_scale[:, b * LANES:(b + 1) * LANES]
+        side[b * LANES:(b + 1) * LANES, :] = jnp.broadcast_to(scales, (LANES, LANES)).T
     columns[...] = jnp.full(columns.shape, LOW, F32)
 
-    p_first()
     z_event(1, 0)
-    p_line(0)
+    for h in (0, 1):
+        below(h)
+        above(h)
+    above(2)
+    above(3)
     z_event(1, 1)
-    p_opposite()
+    across(0)
     z_event(1, 2)
-    p_line(1)
+    below(2)
+    across(1)
+    below(3)
     z_event(1, 3)
+    line(0, 1)
+    line(1, 1)
     z_event(2, 0)
-    p_line(2)
+    across(2)
+    across(3)
+    for h in (0, 1):
+        line(h, 0)
+    for h in (0, 1):
+        line(h, 2)
+    for h in (2, 3):
+        line(h, 0)
     z_event(2, 1)
-    p_line(3)
+    for h in (2, 3):
+        line(h, 2)
+    line(0, 3)
+    line(1, 3)
     z_event(2, 2)
+    line(2, 1)
+    line(3, 1)
     z_event(2, 3)
+    line(2, 3)
+    line(3, 3)
+    for i in range(PIECES):
+        z_event(3, i)
     pltpu.make_async_copy(t_all.at[pl.ds(0, 8)], t_all.at[pl.ds(0, 8)], p_rest).wait()
 
     def features(dz, part):
@@ -237,27 +261,17 @@
                 sim[part, :] = sim[part, :] + dots
 
     tiles = sim.shape[0] // TILE
-    half = tiles // 2
     from_twin(-1)
     from_twin(1)
-    z_event(3, 0)
-    product(-1, 1, 0, half, fresh=True)
-    z_event(3, 1)
-    product(-1, 1, half, tiles, fresh=True)
+    product(-1, 1, 0, tiles, fresh=True)
+    z_event(4, 0)
     from_twin(-2)
     from_twin(2)
-    z_event(3, 2)
-    product(-2, 2, 0, half)
-    z_event(3, 3)
-    product(-2, 2, half, tiles)
+    product(-2, 2, 0, tiles)
+    z_event(4, 1)
     from_twin(-3)
     from_twin(3)
-    z_event(4, 0)
-    z_event(4, 2)
-    product(-3, 3, 0, half)
-    z_event(4, 1)
-    z_event(4, 3)
-    product(-3, 3, half, tiles)
+    product(-3, 3, 0, tiles)
     from_twin(0)
     from_twin(4)
     product(0, 4, 0, tiles)
@@ -394,7 +408,7 @@
         out_specs=(vmem, vmem),
         scratch_shapes=[
             pltpu.VMEM((GROUP, PIECES, depth // PIECES, rows), jnp.bfloat16),
-            pltpu.VMEM((GROUP, 2, depth // 2, cols), jnp.bfloat16),
+            pltpu.VMEM((GROUP, QUARTERS, depth // QUARTERS, cols), jnp.bfloat16),
             pltpu.VMEM((rows, cols), F32),
             pltpu.VMEM((rows, LANES), F32),
             pltpu.VMEM((4, LANES, LANES), F32),
@@ -412,13 +426,13 @@
             dma,
             dma((NZ,)),
             dma,
-            dma((2, 7)),
+            dma((QUARTERS, 7)),
             dma,
             dma((3,)),
             dma((2, 3)),
         ],
         compiler_params=pltpu.CompilerParams(
-            collective_id=0, has_side_effects=True, vmem_limit_bytes=40 * 1024 * 1024
+            collective_id=0, has_side_effects=True, vmem_limit_bytes=55150 * 1024
         ),
         name="mine",
     )(src_codes, src_scale.reshape(1, rows), tgt_codes, tgt_scale.reshape(1, cols))

time: 64.9 us -> 56.4 us (0.87)
  Pallas kernels: 60.3 us -> 53.6 us
  local copies, waits for them, and re-layouts: 3.76 us -> 1.93 us
    pallas_call x1, Pallas kernels: 60.3 us -> 53.6 us  [body(): pl.pallas_call(kernel, out_shape=(jax.ShapeDtypeStruct((4, rows), F32), j...]
    unnamed x8 -> x4, local copies, waits for them, and re-layouts: 3.05 us -> 1.22 us
where the time goes in v3:
time: 56.4 us; the launch traced here: 56.2 us
  Pallas kernels  53.6 us (95%)
  local copies, waits for them, and re-layouts  1.93 us (3%)
  between operations  0.65 us (1%)
    pallas_call x1, Pallas kernels, body(): pl.pallas_call(kernel, out_shape=(jax.ShapeDtypeStruct((4, rows), F32), j...  53.6 us
    unnamed x4, local copies, waits for them, and re-layouts  1.22 us

profile of v3, /device:TPU:1, one launch (start us, length us, event | category | flops | bytes accessed | tf_op | source)
XLA Modules:
  0.0 56.2 jit_solution(1835323554906431530)
XLA Ops:
  0.6 0.0 copy-start
  0.6 0.7 %reshape.10.src_scale = f32[1,1536]{1,0:T(1,128)S(1)} reshape(f32[1536]{0:T(1024)} %param.5) | data formatting | bytes 12288 | tf_op jit(solution)/shard_map/reshape | solution.py:438
  1.3 0.0 copy-done
  1.4 53.6 %mine.1 = (f32[4,1536]{1,0:T(4,128)S(1)}, f32[4,1024]{1,0:T(4,128)S(1)}) custom-call(bf16[64,1536]{1,0:T(8,128)(2,1)} %src_ref.1, f32[1,1536]{1,0:T(1,128)S(1)} %reshape.10.src_scale, bf16[64,1024]{1,0:T(8,128)(2,1)} %tgt_ref.1, f32[1,1024]{1,0:T(1,128)S(1)} %bitcast.1), custom_call_target="tpu_custom_call" | custom-call | tf_op jit(solution)/shard_map/mine/pallas_call | solution.py:401
  55.0 0.6 %copy.8 = f32[4,1536]{1,0:T(4,128)} copy(f32[4,1536]{1,0:T(4,128)S(1)} %get-tuple-element.4) | data formatting | bytes 49152
  55.6 0.6 %copy.9 = f32[4,1024]{1,0:T(4,128)} copy(f32[4,1024]{1,0:T(4,128)S(1)} %get-tuple-element.5) | data formatting | bytes 32768
Async XLA Ops:
  0.6 0.7 %copy-start = (f32[1024]{0:T(1024)S(1)}, f32[1024]{0:T(1024)}, u32[]{:S(2)}) copy-start(f32[1024]{0:T(1024)} %param.7) | copy-start | bytes 12292

commit v4 on v3

--- a/solution.py
+++ b/solution.py
@@ -52,24 +52,37 @@
     return best
 
 
-TAIL = (32, 40, 44, 36)
-
-
-def row_line(k, b):
-    return jnp.where(b < 8, 8 * k + b, TAIL[k] + b - 8)
-
-
-def load_rows(ref):
-    head = [ref[8 * k:8 * k + 8, :] for k in range(4)]
-    first, second = ref[32:40, :], ref[40:48, :]
-    return head, [first, second, pltpu.roll(second, 4, 0), pltpu.roll(first, 4, 0)]
+QUAD = (0, 8, 12, 4)
+
+
+def load8(ref):
+    return [ref[8 * k:8 * k + 8, :] for k in range(4)]
+
+
+def load4(ref):
+    first, second = ref[0:8, :], ref[8:16, :]
+    return [first, second, pltpu.roll(second, 4, 0), pltpu.roll(first, 4, 0)]
+
+
+def store8(ref, best):
+    for k in range(4):
+        ref[8 * k:8 * k + 8, :] = best[k]
+
+
+def store4(ref, best):
+    for k in range(4):
+        ref[QUAD[k]:QUAD[k] + 4, :] = best[k][0:4]
+
+
+HEAD, TAIL, LEFT, RIGHT = range(4)
 
 
 def kernel(
     src_ref, src_scale, tgt_ref, tgt_scale, fwd_ref, bwd_ref,
     s_all, t_all, sim, side, lists, columns,
-    row_out, row_in, pair_out, pair_in,
-    col_out, col_in, col_mean,
+    head_out, head_in, head_pair, head_twin,
+    tail_out, tail_in, tail_pair, tail_twin,
+    left_out, left_in, right_out, right_in, col_mean,
     own_sem, z_send, z_recv, d_send, d_recv, p_send, p_recv, p_rest,
     x_send, x_recv,
 ):
@@ -280,9 +293,11 @@
                        (t_all.at[pl.ds(0, 15)], p_send)):
         pltpu.make_async_copy(slots, slots, sem).wait()
 
-    def sweep(change):
-        @pl.loop(0, row_blocks)
-        def _(b):
+    out = (head_out, tail_out, left_out, right_out)
+    into = (head_in, tail_in, left_in, right_in)
+
+    def sweep(stage, change):
+        def best_of_rows(b):
             def rows(g):
                 return pl.ds(pl.multiple_of(b * LANES + g * 8, 8), 8)
 
@@ -298,69 +313,96 @@
                 for k in range(4):
                     lists[k, g * 8:(g + 1) * 8, :] = best[k]
             turned = [lists[k].T for k in range(4)]
-            best = over_sublanes(tree([[t[g * 8:(g + 1) * 8] for t in turned] for g in range(16)]))
+            return over_sublanes(tree([[t[g * 8:(g + 1) * 8] for t in turned] for g in range(16)]))
+
+        @pl.loop(0, 8)
+        def _(b):
+            best = best_of_rows(b)
             for k in range(4):
-                row_out[pl.ds(row_line(k, b), 1), :] = best[k][0:1]
-            for c in range(col_blocks):
-                lane = pl.ds(c * LANES, LANES)
-                quads = [
-                    sort4([sim[rows(4 * q + g), lane] for g in range(4)]) for q in range(4)
-                ]
-                best = merge4(tree(quads), [columns[c, k] for k in range(4)])
+                head_out[pl.ds(8 * k + b, 1), :] = best[k][0:1]
+
+        send(stage, HEAD)
+
+        @pl.loop(8, row_blocks)
+        def _(b):
+            best = best_of_rows(b)
+            for k in range(4):
+                tail_out[pl.ds(QUAD[k] + b - 8, 1), :] = best[k][0:1]
+
+        send(stage, TAIL)
+
+        for part in (LEFT, RIGHT):
+            first = 0 if part == LEFT else 4
+
+            @pl.loop(0, row_blocks)
+            def _(b, first=first):
+                for c in range(first, first + 4):
+                    lane = pl.ds(c * LANES, LANES)
+                    quads = [
+                        sort4([
+                            sim[pl.ds(pl.multiple_of(b * LANES + (4 * q + g) * 8, 8), 8), lane]
+                            for g in range(4)
+                        ])
+                        for q in range(4)
+                    ]
+                    best = merge4(tree(quads), [columns[c, k] for k in range(4)])
+                    for k in range(4):
+                        columns[c, k] = best[k]
+
+            for c in range(4):
+                best = over_sublanes([columns[first + c, k] for k in range(4)])
                 for k in range(4):
-                    columns[c, k] = best[k]
-
-        for c in range(col_blocks):
-            best = over_sublanes([columns[c, k] for k in range(4)])
-            for k in range(4):
-                col_out[k, c:c + 1, :] = best[k][0:1]
-
-    def exchange(stage):
-        sends = []
-        for r in range(1, NZ):
-            sends.append(pltpu.make_async_remote_copy(
-                src_ref=row_out, dst_ref=row_in.at[stage, r - 1],
-                send_sem=x_send.at[0], recv_sem=x_recv.at[stage, 0],
-                device_id=(src_me, at_z(r)), device_id_type=MESH,
-            ))
-        for r in range(1, GROUP):
-            sends.append(pltpu.make_async_remote_copy(
-                src_ref=col_out, dst_ref=col_in.at[stage, r - 1],
-                send_sem=x_send.at[1], recv_sem=x_recv.at[stage, 1],
-                device_id=(around(src_me, r, GROUP), tgt_me), device_id_type=MESH,
-            ))
-        for copy in sends:
-            copy.start()
-        row_slots, col_slots = row_in.at[stage], col_in.at[stage]
-
-        pltpu.make_async_copy(row_slots, row_slots, x_recv.at[stage, 0]).wait()
-        ours = [load_rows(row_out)] + [load_rows(row_in.at[stage, r]) for r in range(NZ - 1)]
-        head, tail = tree([v[0] for v in ours]), tree([v[1] for v in ours])
-        for k in range(4):
-            pair_out[8 * k:8 * k + 8, :] = head[k]
-            pair_out[TAIL[k]:TAIL[k] + 4, :] = tail[k][0:4]
-        pair = pltpu.make_async_remote_copy(
-            src_ref=pair_out, dst_ref=pair_in.at[stage],
-            send_sem=x_send.at[2], recv_sem=x_recv.at[stage, 2],
+                    out[part][QUAD[k] + c:QUAD[k] + c + 1, :] = best[k][0:1]
+            send(stage, part)
+
+    def send(stage, part):
+        for r in range(1, NZ if part in (HEAD, TAIL) else GROUP):
+            device = (
+                (src_me, at_z(r)) if part in (HEAD, TAIL) else (around(src_me, r, GROUP), tgt_me)
+            )
+            pltpu.make_async_remote_copy(
+                src_ref=out[part], dst_ref=into[part].at[stage, r - 1],
+                send_sem=x_send.at[part], recv_sem=x_recv.at[stage, part],
+                device_id=device, device_id_type=MESH,
+            ).start()
+
+    def gathered(stage, part):
+        slots = into[part].at[stage]
+        pltpu.make_async_copy(slots, slots, x_recv.at[stage, part]).wait()
+        load = load8 if part == HEAD else load4
+        count = into[part].shape[1]
+        best = tree([load(out[part])] + [load(into[part].at[stage, r]) for r in range(count)])
+        return best
+
+    def sent(stage):
+        for part in (HEAD, TAIL, LEFT, RIGHT):
+            slots = into[part].at[stage]
+            pltpu.make_async_copy(slots, slots, x_send.at[part]).wait()
+
+    def twin_copy(stage, part):
+        mine, theirs = ((head_pair, head_twin), (tail_pair, tail_twin))[part]
+        return pltpu.make_async_remote_copy(
+            src_ref=mine, dst_ref=theirs.at[stage],
+            send_sem=x_send.at[4 + part], recv_sem=x_recv.at[stage, 4 + part],
             device_id=twin, device_id_type=MESH,
         )
-        pair.start()
-
-        pltpu.make_async_copy(col_slots, col_slots, x_recv.at[stage, 1]).wait()
-        everyone = [[col_out[k] for k in range(4)]]
-        everyone += [[col_in[stage, r, k] for k in range(4)] for r in range(GROUP - 1)]
-        col_best = tree(everyone)
-
-        pair.wait_recv()
-        other_head, other_tail = load_rows(pair_in.at[stage])
-        head, tail = merge4(head, other_head), merge4(tail, other_tail)
-        pair.wait_send()
-        pltpu.make_async_copy(row_slots, row_slots, x_send.at[0]).wait()
-        pltpu.make_async_copy(col_slots, col_slots, x_send.at[1]).wait()
-        return head, tail, col_best
-
-    def line_of(head, tail, b):
-        return head[b:b + 1] if b < 8 else tail[b - 8:b - 7]
+
+    def combined(stage, use_head, use_tail, use_cols):
+        head = gathered(stage, HEAD)
+        store8(head_pair, head)
+        twin_copy(stage, HEAD).start()
+        tail = gathered(stage, TAIL)
+        store4(tail_pair, tail)
+        twin_copy(stage, TAIL).start()
+        use_cols(0, gathered(stage, LEFT))
+        twin_copy(stage, HEAD).wait_recv()
+        use_head(merge4(head, load8(head_twin.at[stage])))
+        twin_copy(stage, TAIL).wait_recv()
+        use_tail(merge4(tail, load4(tail_twin.at[stage])))
+        use_cols(4, gathered(stage, RIGHT))
+        for part in (HEAD, TAIL):
+            twin_copy(stage, part).wait_send()
+        sent(stage)
 
     def scaled(value, beside, c):
         return value * beside * tgt_scale[:, c * LANES:(c + 1) * LANES]
@@ -368,27 +410,43 @@
     def half_mean(best):
         return (best[0] + best[1] + best[2] + best[3]) * 0.125
 
-    sweep(scaled)
-    head, tail, col_best = exchange(0)
-
-    head, tail, beneath = half_mean(head), half_mean(tail), half_mean(col_best)
-    for b in range(row_blocks):
-        line = line_of(head, tail, b)
-        side[b * LANES:(b + 1) * LANES, :] = jnp.broadcast_to(line, (LANES, LANES)).T
-    for c in range(col_blocks):
-        col_mean[c] = jnp.broadcast_to(beneath[c:c + 1], (8, LANES))
+    def rows_mean(first, count):
+        def use(best):
+            mean = half_mean(best)
+            for b in range(count):
+                at = (first + b) * LANES
+                side[at:at + LANES, :] = jnp.broadcast_to(mean[b:b + 1], (LANES, LANES)).T
+        return use
+
+    def cols_mean(first, best):
+        mean = half_mean(best)
+        for c in range(4):
+            col_mean[first + c] = jnp.broadcast_to(mean[c:c + 1], (8, LANES))
+
+    sweep(0, scaled)
+    combined(0, rows_mean(0, 8), rows_mean(8, row_blocks - 8), cols_mean)
+
     columns[...] = jnp.full(columns.shape, LOW, F32)
 
     def margin(value, beside, c):
         return value / (beside + col_mean[c])
 
-    sweep(margin)
-    head, tail, col_best = exchange(1)
-    for k in range(4):
-        for b in range(row_blocks):
-            fwd_ref[k:k + 1, b * LANES:(b + 1) * LANES] = line_of(head[k], tail[k], b)
-        for c in range(col_blocks):
-            bwd_ref[k:k + 1, c * LANES:(c + 1) * LANES] = col_best[k][c:c + 1]
+    def rows_out(first, count):
+        def use(best):
+            for k in range(4):
+                for b in range(count):
+                    at = (first + b) * LANES
+                    fwd_ref[k:k + 1, at:at + LANES] = best[k][b:b + 1]
+        return use
+
+    def cols_out(first, best):
+        for k in range(4):
+            for c in range(4):
+                at = (first + c) * LANES
+                bwd_ref[k:k + 1, at:at + LANES] = best[k][c:c + 1]
+
+    sweep(1, margin)
+    combined(1, rows_out(0, 8), rows_out(8, row_blocks - 8), cols_out)
 
 
 def body(src_codes, src_scale, tgt_codes, tgt_scale):
@@ -413,12 +471,18 @@
             pltpu.VMEM((rows, LANES), F32),
             pltpu.VMEM((4, LANES, LANES), F32),
             pltpu.VMEM((col_blocks, 4, 8, LANES), F32),
-            pltpu.VMEM((48, LANES), F32),
-            pltpu.VMEM((2, NZ - 1, 48, LANES), F32),
-            pltpu.VMEM((48, LANES), F32),
-            pltpu.VMEM((2, 48, LANES), F32),
-            pltpu.VMEM((4, 8, LANES), F32),
-            pltpu.VMEM((2, GROUP - 1, 4, 8, LANES), F32),
+            pltpu.VMEM((32, LANES), F32),
+            pltpu.VMEM((2, NZ - 1, 32, LANES), F32),
+            pltpu.VMEM((32, LANES), F32),
+            pltpu.VMEM((2, 32, LANES), F32),
+            pltpu.VMEM((16, LANES), F32),
+            pltpu.VMEM((2, NZ - 1, 16, LANES), F32),
+            pltpu.VMEM((16, LANES), F32),
+            pltpu.VMEM((2, 16, LANES), F32),
+            pltpu.VMEM((16, LANES), F32),
+            pltpu.VMEM((2, GROUP - 1, 16, LANES), F32),
+            pltpu.VMEM((16, LANES), F32),
+            pltpu.VMEM((2, GROUP - 1, 16, LANES), F32),
             pltpu.VMEM((col_blocks, 8, LANES), F32),
             dma((2, 4)),
             dma,
@@ -428,8 +492,8 @@
             dma,
             dma((QUARTERS, 7)),
             dma,
-            dma((3,)),
-            dma((2, 3)),
+            dma((6,)),
+            dma((2, 6)),
         ],
         compiler_params=pltpu.CompilerParams(
             collective_id=0, has_side_effects=True, vmem_limit_bytes=55150 * 1024

time: 56.4 us -> 54.3 us (0.963)
  Pallas kernels: 53.6 us -> 51.5 us
    pallas_call x1, Pallas kernels: 53.6 us -> 51.5 us  [body(): pl.pallas_call(kernel, out_shape=(jax.ShapeDtypeStruct((4, rows), F32), j...]
where the time goes in v4:
time: 54.3 us; the launch traced here: 54.1 us
  Pallas kernels  51.5 us (95%)
  local copies, waits for them, and re-layouts  1.93 us (4%)
  between operations  0.65 us (1%)
    pallas_call x1, Pallas kernels, body(): pl.pallas_call(kernel, out_shape=(jax.ShapeDtypeStruct((4, rows), F32), j...  51.5 us
    unnamed x4, local copies, waits for them, and re-layouts  1.22 us

profile of v4, /device:TPU:1, one launch (start us, length us, event | category | flops | bytes accessed | tf_op | source)
XLA Modules:
  0.0 54.1 jit_solution(833132478876773588)
XLA Ops:
  0.6 0.0 copy-start
  0.6 0.7 %reshape.10.src_scale = f32[1,1536]{1,0:T(1,128)S(1)} reshape(f32[1536]{0:T(1024)} %param.5) | data formatting | bytes 12288 | tf_op jit(solution)/shard_map/reshape | solution.py:502
  1.3 0.0 copy-done
  1.4 51.5 %mine.1 = (f32[4,1536]{1,0:T(4,128)S(1)}, f32[4,1024]{1,0:T(4,128)S(1)}) custom-call(bf16[64,1536]{1,0:T(8,128)(2,1)} %src_ref.1, f32[1,1536]{1,0:T(1,128)S(1)} %reshape.10.src_scale, bf16[64,1024]{1,0:T(8,128)(2,1)} %tgt_ref.1, f32[1,1024]{1,0:T(1,128)S(1)} %bitcast.1), custom_call_target="tpu_custom_call" | custom-call | tf_op jit(solution)/shard_map/mine/pallas_call | solution.py:459
  52.9 0.6 %copy.8 = f32[4,1536]{1,0:T(4,128)} copy(f32[4,1536]{1,0:T(4,128)S(1)} %get-tuple-element.4) | data formatting | bytes 49152
  53.5 0.6 %copy.9 = f32[4,1024]{1,0:T(4,128)} copy(f32[4,1024]{1,0:T(4,128)S(1)} %get-tuple-element.5) | data formatting | bytes 32768
Async XLA Ops:
  0.6 0.7 %copy-start = (f32[1024]{0:T(1024)S(1)}, f32[1024]{0:T(1024)}, u32[]{:S(2)}) copy-start(f32[1024]{0:T(1024)} %param.7) | copy-start | bytes 12292

commit v5 on v4

--- a/solution.py
+++ b/solution.py
@@ -315,7 +315,7 @@
             turned = [lists[k].T for k in range(4)]
             return over_sublanes(tree([[t[g * 8:(g + 1) * 8] for t in turned] for g in range(16)]))
 
-        @pl.loop(0, 8)
+        @pl.loop(0, 8, unroll=4)
         def _(b):
             best = best_of_rows(b)
             for k in range(4):
@@ -323,7 +323,7 @@
 
         send(stage, HEAD)
 
-        @pl.loop(8, row_blocks)
+        @pl.loop(8, row_blocks, unroll=4)
         def _(b):
             best = best_of_rows(b)
             for k in range(4):

time: 54.3 us -> 52.5 us (0.967)
  Pallas kernels: 51.5 us -> 49.7 us
    pallas_call x1, Pallas kernels: 51.5 us -> 49.7 us  [body(): pl.pallas_call(kernel, out_shape=(jax.ShapeDtypeStruct((4, rows), F32), j...]
where the time goes in v5:
time: 52.5 us; the launch traced here: 52.3 us
  Pallas kernels  49.7 us (95%)
  local copies, waits for them, and re-layouts  1.93 us (4%)
  between operations  0.65 us (1%)
    pallas_call x1, Pallas kernels, body(): pl.pallas_call(kernel, out_shape=(jax.ShapeDtypeStruct((4, rows), F32), j...  49.7 us
    unnamed x4, local copies, waits for them, and re-layouts  1.22 us

profile of v5, /device:TPU:1, one launch (start us, length us, event | category | flops | bytes accessed | tf_op | source)
XLA Modules:
  0.0 52.3 jit_solution(3481667647757020694)
XLA Ops:
  0.6 0.0 copy-start
  0.6 0.7 %reshape.10.src_scale = f32[1,1536]{1,0:T(1,128)S(1)} reshape(f32[1536]{0:T(1024)} %param.5) | data formatting | bytes 12288 | tf_op jit(solution)/shard_map/reshape | solution.py:502
  1.3 0.0 copy-done
  1.4 49.7 %mine.1 = (f32[4,1536]{1,0:T(4,128)S(1)}, f32[4,1024]{1,0:T(4,128)S(1)}) custom-call(bf16[64,1536]{1,0:T(8,128)(2,1)} %src_ref.1, f32[1,1536]{1,0:T(1,128)S(1)} %reshape.10.src_scale, bf16[64,1024]{1,0:T(8,128)(2,1)} %tgt_ref.1, f32[1,1024]{1,0:T(1,128)S(1)} %bitcast.1), custom_call_target="tpu_custom_call" | custom-call | tf_op jit(solution)/shard_map/mine/pallas_call | solution.py:459
  51.1 0.6 %copy.8 = f32[4,1536]{1,0:T(4,128)} copy(f32[4,1536]{1,0:T(4,128)S(1)} %get-tuple-element.4) | data formatting | bytes 49152
  51.7 0.6 %copy.9 = f32[4,1024]{1,0:T(4,128)} copy(f32[4,1024]{1,0:T(4,128)S(1)} %get-tuple-element.5) | data formatting | bytes 32768
Async XLA Ops:
  0.6 0.7 %copy-start = (f32[1024]{0:T(1024)S(1)}, f32[1024]{0:T(1024)}, u32[]{:S(2)}) copy-start(f32[1024]{0:T(1024)} %param.7) | copy-start | bytes 12292

commit v6 on v5

--- a/solution.py
+++ b/solution.py
@@ -315,7 +315,7 @@
             turned = [lists[k].T for k in range(4)]
             return over_sublanes(tree([[t[g * 8:(g + 1) * 8] for t in turned] for g in range(16)]))
 
-        @pl.loop(0, 8, unroll=4)
+        @pl.loop(0, 8, unroll=8)
         def _(b):
             best = best_of_rows(b)
             for k in range(4):
@@ -356,12 +356,15 @@
             send(stage, part)
 
     def send(stage, part):
-        for r in range(1, NZ if part in (HEAD, TAIL) else GROUP):
-            device = (
-                (src_me, at_z(r)) if part in (HEAD, TAIL) else (around(src_me, r, GROUP), tgt_me)
-            )
+        if part in (HEAD, TAIL):
+            devices = [(src_me, at_z(r)) for r in (4, 3, 5, 2, 6, 1, 7)]
+        else:
+            steps = [(dx, dy) for dx in range(NX) for dy in range(NY) if dx or dy]
+            steps.sort(key=lambda step: -sum(min(v, 4 - v) for v in step))
+            devices = [(at_xy(*step), tgt_me) for step in steps]
+        for slot, device in enumerate(devices):
             pltpu.make_async_remote_copy(
-                src_ref=out[part], dst_ref=into[part].at[stage, r - 1],
+                src_ref=out[part], dst_ref=into[part].at[stage, slot],
                 send_sem=x_send.at[part], recv_sem=x_recv.at[stage, part],
                 device_id=device, device_id_type=MESH,
             ).start()

time: 52.5 us -> 51.6 us (0.983)
  Pallas kernels: 49.7 us -> 48.8 us
    pallas_call x1, Pallas kernels: 49.7 us -> 48.8 us  [body(): pl.pallas_call(kernel, out_shape=(jax.ShapeDtypeStruct((4, rows), F32), j...]
where the time goes in v6:
time: 51.6 us; the launch traced here: 51.4 us
  Pallas kernels  48.8 us (95%)
  local copies, waits for them, and re-layouts  1.93 us (4%)
  between operations  0.65 us (1%)
    pallas_call x1, Pallas kernels, body(): pl.pallas_call(kernel, out_shape=(jax.ShapeDtypeStruct((4, rows), F32), j...  48.8 us
    unnamed x4, local copies, waits for them, and re-layouts  1.22 us

profile of v6, /device:TPU:1, one launch (start us, length us, event | category | flops | bytes accessed | tf_op | source)
XLA Modules:
  0.0 51.4 jit_solution(2040889169081221154)
XLA Ops:
  0.6 0.0 copy-start
  0.6 0.7 %reshape.10.src_scale = f32[1,1536]{1,0:T(1,128)S(1)} reshape(f32[1536]{0:T(1024)} %param.5) | data formatting | bytes 12288 | tf_op jit(solution)/shard_map/reshape | solution.py:505
  1.3 0.0 copy-done
  1.4 48.8 %mine.1 = (f32[4,1536]{1,0:T(4,128)S(1)}, f32[4,1024]{1,0:T(4,128)S(1)}) custom-call(bf16[64,1536]{1,0:T(8,128)(2,1)} %src_ref.1, f32[1,1536]{1,0:T(1,128)S(1)} %reshape.10.src_scale, bf16[64,1024]{1,0:T(8,128)(2,1)} %tgt_ref.1, f32[1,1024]{1,0:T(1,128)S(1)} %bitcast.1), custom_call_target="tpu_custom_call" | custom-call | tf_op jit(solution)/shard_map/mine/pallas_call | solution.py:462
  50.2 0.6 %copy.8 = f32[4,1536]{1,0:T(4,128)} copy(f32[4,1536]{1,0:T(4,128)S(1)} %get-tuple-element.4) | data formatting | bytes 49152
  50.8 0.6 %copy.9 = f32[4,1024]{1,0:T(4,128)} copy(f32[4,1024]{1,0:T(4,128)S(1)} %get-tuple-element.5) | data formatting | bytes 32768
Async XLA Ops:
  0.6 0.7 %copy-start = (f32[1024]{0:T(1024)S(1)}, f32[1024]{0:T(1024)}, u32[]{:S(2)}) copy-start(f32[1024]{0:T(1024)} %param.7) | copy-start | bytes 12292
